TPU v7x, 32 devices: a whole 2x2x4 slice. The times are simulated.
32 devices in a mesh: ta: 8 (over y, x, core), gz: 4 (over z).
Axes of the slice: x: 2, y: 2, z: 4, core: 2. Of those that a mesh axis runs over, the one named last changes fastest.
Arguments:
- spinor: float32 [2, 4, 3, 16, 8, 768], P(None, None, None, 'ta', 'gz'), may hold values from -3 to 3
- links: float32 [4, 2, 3, 3, 16, 8, 768], P(None, None, None, None, 'ta', 'gz'), may hold values from -3.5 to 3.5
- clover: float32 [2, 2, 6, 6, 16, 8, 768], P(None, None, None, None, 'ta', 'gz'), may hold values from -1.2 to 1.2
Outputs:
- applied: float32 [2, 4, 3, 16, 8, 768], P(None, None, None, 'ta', 'gz')
- force: float32 [4, 2, 3, 3, 16, 8, 768], P(None, None, None, None, 'ta', 'gz')
All inputs are finite; a program needn't handle non-finite values.
Results may differ from a plain program's by a relative error of at most 0.0001.
Values sent between devices are 32-bit elements; how exact they have to be, the bound alone decides.
A program may use at most 64 MiB of HBM per device.

v0:
```python
import jax
import jax.numpy as jnp
from jax import lax
from jax.sharding import PartitionSpec as P

NY = 12
NX = 64


bare_mass = -0.25
gamma_table = (
    ((3, 0.0, -1.0), (2, 0.0, -1.0), (1, 0.0, 1.0), (0, 0.0, 1.0)),
    ((3, -1.0, 0.0), (2, 1.0, 0.0), (1, 1.0, 0.0), (0, -1.0, 0.0)),
    ((2, 0.0, -1.0), (3, 0.0, 1.0), (0, 0.0, 1.0), (1, 0.0, -1.0)),
    ((2, 1.0, 0.0), (3, 1.0, 0.0), (0, 1.0, 0.0), (1, 1.0, 0.0)),
)


def with_halo(block, sides, width):
    for axis, dim in sides:
        count = lax.axis_size(axis)
        forward = [(i, i + 1) for i in range(count - 1)]
        forward.append((count - 1, 0))
        backward = [(target, source) for source, target in forward]
        low = lax.ppermute(
            lax.slice_in_dim(block, block.shape[dim] - width, None, axis=dim), axis, forward
        )
        high = lax.ppermute(lax.slice_in_dim(block, 0, width, axis=dim), axis, backward)
        block = jnp.concatenate([low, block, high], axis=dim)
    return block


def passed_along(value, axis, steps):
    count = lax.axis_size(axis)
    pairs = [(source, (source + steps) % count) for source in range(count)]
    return lax.ppermute(value, axis, pairs)


def apply_gamma(hop_dir, field):
    parts_re = []
    parts_im = []
    for spin_row in range(4):
        source, phase_re, phase_im = gamma_table[hop_dir][spin_row]
        source_re = field[0, source]
        source_im = field[1, source]
        if phase_im == 0.0:
            parts_re.append(phase_re * source_re)
            parts_im.append(phase_re * source_im)
        else:
            parts_re.append(-phase_im * source_im)
            parts_im.append(phase_im * source_re)
    return jnp.stack([jnp.stack(parts_re), jnp.stack(parts_im)])


def project(hop_dir, field, sign):
    return field + sign * apply_gamma(hop_dir, field)


def color_apply(link, field, dagger):
    link_re = link[0]
    link_im = link[1]
    if dagger:
        link_re = jnp.swapaxes(link_re, 0, 1)
        link_im = -jnp.swapaxes(link_im, 0, 1)
    matrix_re = link_re[None]
    matrix_im = link_im[None]
    field_re = field[0][:, None]
    field_im = field[1][:, None]
    out_re = jnp.sum(matrix_re * field_re - matrix_im * field_im, axis=2)
    out_im = jnp.sum(matrix_re * field_im + matrix_im * field_re, axis=2)
    return jnp.stack([out_re, out_im])


def clover_apply(clover, field):
    halves = field.reshape((2, 2, 6) + field.shape[3:])
    field_re = halves[0][:, None]
    field_im = halves[1][:, None]
    out_re = jnp.sum(clover[0] * field_re - clover[1] * field_im, axis=2)
    out_im = jnp.sum(clover[0] * field_im + clover[1] * field_re, axis=2)
    return jnp.stack([out_re, out_im]).reshape(field.shape)


def spin_outer(left, right):
    left_re = left[0][:, :, None]
    left_im = left[1][:, :, None]
    right_re = right[0][:, None]
    right_im = right[1][:, None]
    out_re = jnp.sum(left_re * right_re + left_im * right_im, axis=0)
    out_im = jnp.sum(left_im * right_re - left_re * right_im, axis=0)
    return jnp.stack([out_re, out_im])


def color_product(first, second):
    first_re = first[0][:, :, None]
    first_im = first[1][:, :, None]
    second_re = second[0][None]
    second_im = second[1][None]
    out_re = jnp.sum(first_re * second_re - first_im * second_im, axis=1)
    out_im = jnp.sum(first_re * second_im + first_im * second_re, axis=1)
    return jnp.stack([out_re, out_im])


def traceless(matrix):
    mat_re = matrix[0]
    mat_im = matrix[1]
    anti_re = 0.5 * (mat_re - jnp.swapaxes(mat_re, 0, 1))
    anti_im = 0.5 * (mat_im + jnp.swapaxes(mat_im, 0, 1))
    trace_third = (mat_im[0, 0] + mat_im[1, 1] + mat_im[2, 2]) / 3.0
    identity = jnp.eye(3, dtype=jnp.float32).reshape((3, 3) + (1,) * (mat_re.ndim - 2))
    return jnp.stack([anti_re, anti_im - identity * trace_third])


def along_plane(field, hop_dir, step):
    shape = field.shape
    grid = field.reshape(shape[:-1] + (NY, NX))
    if hop_dir == 0:
        grid = jnp.roll(grid, -step, axis=-1)
    else:
        grid = jnp.roll(grid, -step, axis=-2)
    return grid.reshape(shape)


def slab(field, start, stop, dimension):
    return lax.slice_in_dim(field, start, stop, axis=dimension)


def body(spinor, links, clover):
    t_slices = spinor.shape[3]
    z_slices = spinor.shape[4]
    t_place = lax.axis_index("ta")
    t_count = lax.axis_size("ta")
    low_sign = jnp.where(t_place == 0, -1.0, 1.0).astype(jnp.float32)
    high_sign = jnp.where(t_place == t_count - 1, -1.0, 1.0).astype(jnp.float32)
    forward_half = []
    hopping = jnp.zeros_like(spinor)
    for hop_dir in (0, 1):
        ahead_proj = project(hop_dir, along_plane(spinor, hop_dir, 1), -1.0)
        forward_half.append(ahead_proj)
        behind = along_plane(spinor, hop_dir, -1)
        back_link = along_plane(links[hop_dir], hop_dir, -1)
        hopping = (
            hopping
            + color_apply(links[hop_dir], ahead_proj, False)
            + color_apply(back_link, project(hop_dir, behind, 1.0), True)
        )
    extended = with_halo(spinor, (("ta", 3), ("gz", 4)), 1)
    link_t_low = passed_along(links[3][:, :, :, t_slices - 1 :], "ta", 1)
    link_z_low = passed_along(links[2][:, :, :, :, z_slices - 1 :], "gz", 1)
    z_upper = extended[:, :, :, 1 : t_slices + 1, z_slices + 1 :]
    z_lower = extended[:, :, :, 1 : t_slices + 1, :1]
    t_upper = extended[:, :, :, t_slices + 1 :, 1 : z_slices + 1] * high_sign
    t_lower = extended[:, :, :, :1, 1 : z_slices + 1] * low_sign
    for hop_dir, dimension, upper_face, lower_face, link_face in (
        (2, 4, z_upper, z_lower, link_z_low),
        (3, 3, t_upper, t_lower, link_t_low),
    ):
        size_here = spinor.shape[dimension]
        ahead = jnp.concatenate([slab(spinor, 1, size_here, dimension), upper_face], axis=dimension)
        behind = jnp.concatenate(
            [lower_face, slab(spinor, 0, size_here - 1, dimension)], axis=dimension
        )
        back_link = jnp.concatenate(
            [link_face, slab(links[hop_dir], 0, size_here - 1, dimension)], axis=dimension
        )
        ahead_proj = project(hop_dir, ahead, -1.0)
        forward_half.append(ahead_proj)
        hopping = (
            hopping
            + color_apply(links[hop_dir], ahead_proj, False)
            + color_apply(back_link, project(hop_dir, behind, 1.0), True)
        )
    applied = (4.0 + bare_mass) * spinor + clover_apply(clover, spinor) - 0.5 * hopping
    applied_t = passed_along(applied[:, :, :, :1], "ta", -1) * high_sign
    applied_z = passed_along(applied[:, :, :, :, :1], "gz", -1)
    ahead_applied = [
        along_plane(applied, 0, 1),
        along_plane(applied, 1, 1),
        jnp.concatenate([applied[:, :, :, :, 1:], applied_z], axis=4),
        jnp.concatenate([applied[:, :, :, 1:], applied_t], axis=3),
    ]
    forces = []
    for hop_dir in range(4):
        summed = spin_outer(forward_half[hop_dir], applied) + spin_outer(
            project(hop_dir, ahead_applied[hop_dir], 1.0), spinor
        )
        forces.append(traceless(color_product(links[hop_dir], summed)))
    return (applied, jnp.stack(forces))


def solution(mesh):
    return jax.shard_map(
        body,
        mesh=mesh,
        in_specs=(
            P(None, None, None, "ta", "gz", None),
            P(None, None, None, None, "ta", "gz", None),
            P(None, None, None, None, "ta", "gz", None),
        ),
        out_specs=(
            P(None, None, None, "ta", "gz", None),
            P(None, None, None, None, "ta", "gz", None),
        ),
        check_vma=False,
    )
```

profile of v0, /device:TPU:0, one launch (start us, length us, event | category | flops | bytes accessed | tf_op | source)
XLA Modules:
  0.0 87.4 jit_solution(9460520527098681229)
XLA Ops:
  0.6 1.1 %fusion.163 = (f32[2,4,3,1,2,768]{5,4,3,2,1,0:T(2,128)S(1)}, f32[2,4,3,1,2,768]{5,4,3,2,1,0:T(2,128)S(1)}) fusion(f32[2,4,3,2,2,768]{5,4,3,2,1,0:T(2,128)} %param.3), kind=kLoop, calls=%fused_computation.523 | loop fusion | bytes 589824 | tf_op jit(solution)/shard_map/slice | solution.py:28
  1.7 0.7 copy.477
  2.4 3.4 %collective-permute-start.1 = (f32[2,4,3,1,2,768]{5,1,4,3,2,0:T(4,128)}, f32[2,4,3,1,2,768]{5,1,4,3,2,0:T(4,128)}, u32[]{:S(2)}, u32[]{:S(2)}) collective-permute-start(f32[2,4,3,1,2,768]{5,1,4,3,2,0:T(4,128)} %copy.477), channel_id=1, source_target_pairs={{4,0},{8,4},{12,8},{16,12},{20,16},{24,20},{28,24},{0,28},{5,1},{9... | collective-permute-start | bytes 442376 | tf_op jit(solution)/shard_map/ppermute | solution.py:28
  5.8 0.7 copy.476
  6.5 1.1 %slice_bitcast_fusion = (f32[2,3,3,2,2,768]{5,4,3,2,1,0:T(2,128)S(1)}, f32[2,3,3,2,2,768]{5,4,3,2,1,0:T(2,128)S(1)}, f32[1,2,3,3,2,2,768]{6,5,4,3,2,1,0:T(2,128)}, f32[1,2,3,3,2,2,768]{6,5,4,3,2,1,0:T(2,128)}) fusion(f32[4,2,3,3,2,2,768]{6,5,4,3,2,1,0:T(2,128)S(1)} %copy-done.1), kind=kLoop, calls=%fused_computation.205 | loop fusion | bytes 1769472 | tf_op jit(solution)/shard_map/squeeze | solution.py:169
  7.6 0.9 fusion.167
  8.4 1.6 %collective-permute-start.3 = (f32[2,3,3,2,1,768]{5,4,3,2,1,0:T(1,128)}, f32[2,3,3,2,1,768]{5,4,3,2,1,0:T(1,128)}, u32[]{:S(2)}, u32[]{:S(2)}) collective-permute-start(f32[2,3,3,2,1,768]{5,4,3,2,1,0:T(1,128)} %get-tuple-element.234), channel_id=1, source_target_pairs={{0,1},{1,2},{2,3},{3,0},{4,5},{5,6},{6,7},{7,4},{8,9},{9,10},{10,1... | collective-permute-start | bytes 331784 | tf_op jit(solution)/shard_map/ppermute | solution.py:36
  10.0 0.7 fusion.166
  10.7 0.9 %slice_bitcast_fusion.45 = (f32[4,3,2,2,768]{4,3,2,1,0:T(2,128)}, f32[4,3,2,2,768]{4,3,2,1,0:T(2,128)}, f32[1,4,3,2,2,768]{5,4,3,2,1,0:T(2,128)S(1)}, f32[1,4,3,2,2,768]{5,4,3,2,1,0:T(2,128)S(1)}) fusion(f32[2,4,3,2,2,768]{5,4,3,2,1,0:T(2,128)S(1)} %copy-done), kind=kLoop, calls=%fused_computation.513 | loop fusion | bytes 884736 | tf_op jit(solution)/shard_map/mul | solution.py:88
  12.6 0.9 %slice_bitcast_fusion.37 = (f32[3,3,2,2,768]{4,3,2,1,0:T(2,128)}, f32[3,3,2,2,768]{4,3,2,1,0:T(2,128)}, f32[3,3,2,2,768]{4,3,2,1,0:T(2,128)}, f32[3,3,2,2,768]{4...) fusion(f32[4,2,3,3,2,2,768]{6,5,4,3,2,1,0:T(2,128)S(1)} %copy-d, ...), kind=kLoop, calls=%fused_computation.304 | loop fusion | bytes 1769472 | tf_op jit(solution)/shard_map/mul | solution.py:69
  13.5 0.7 fusion.154
  14.4 0.9 %fusion.162 = (f32[2,4,3,2,1,768]{5,4,3,2,1,0:T(1,128)}, f32[2,4,3,2,1,768]{5,4,3,2,1,0:T(1,128)}) fusion(f32[2,4,3,2,2,768]{5,4,3,2,1,0:T(2,128)S(1)} %copy-done), kind=kLoop, calls=%fused_computation.522 | loop fusion | bytes 589824 | tf_op jit(solution)/shard_map/slice | solution.py:124
  15.8 1.3 %fusion.1 = (f32[2,6,2,2,768]{4,3,2,1,0:T(2,128)S(1)}, f32[2,6,2,2,768]{4,3,2,1,0:T(2,128)S(1)}) fusion(f32[2,2,6,6,2,2,768]{6,5,4,3,2,1,0:T(2,128)S(1)} %copy-done.3, f32[2,6,2,2,768]{4,3,2,1,0:T(2,128)S(1)} %bitcast.676, f32[2,6,2,2,768]{4,3,2,1,0:T(2,128)S(1)} %bitcast.675), kind=kLoop, calls=%fused_computation.4 | loop fusion | flops 1695744 | bytes 2359296 | tf_op jit(solution)/shard_map/reduce_sum | solution.py:78
  17.1 0.7 copy.181
  17.8 0.7 copy.180
  18.9 1.1 %reshape.579 = f32[2,4,3,2,2,768]{5,4,3,2,1,0:T(2,128)} reshape(f32[2,4,3,2,2,12,64]{6,5,4,3,2,1,0:T(8,128)S(1)} %get-tuple-element.244) | data formatting | bytes 589824 | tf_op jit(solution)/shard_map/reshape | solution.py:120
  20.0 1.0 %fusion.165 = (f32[1,1,3,2,2,768]{5,4,3,2,1,0:T(2,128)S(1)}, f32[1,1,3,2,2,768]{5,4,3,2,1,0:T(2,128)S(1)}, f32[1,1,3,2,2,768]{5,4,3,2,1,0:T(2,128)S(1)}, f32[1,1...) fusion(f32[2,4,3,2,2,768]{5,4,3,2,1,0:T(2,128)} %reshape.579), kind=kLoop, calls=%fused_computation.525 | loop fusion | flops 36864 | bytes 589824 | tf_op jit(solution)/shard_map/slice | solution.py:45
  21.8 0.7 slice_bitcast_fusion.27
  23.8 0.7 slice_bitcast_fusion.25
  25.3 0.8 squeeze.18
  26.1 0.8 neg.37
  26.9 1.2 %pad_maximum_fusion.3 = (f32[2,4,3,2,2,12,64]{6,5,4,3,2,1,0:T(8,128)S(1)}, f32[2,4,3,2,2,12,64]{6,5,4,3,2,1,0:T(8,128)S(1)}) fusion(f32[2,4,3,2,2,1,64]{6,5,4,3,2,1,0:T(1,128)} %get-tuple-element.75, f32[2,4,3,2,2,11,64]{6,5,4,3,2,1,0:T(8,128)S(1)} %get-tuple-element.77, f32[2,4,3,2,2,11,64]{6,5,4,3,2,1,0:T(8,128)S(1)} %get-tuple-element.76, ...), kind=kLoop, calls=%fused_computation.11 | loop fusion | flops 147456 | bytes 1179648 | tf_op jit(solution)/shard_map/jit(_roll_static)/concatenate | solution.py:119
  31.5 0.9 %copy.478 = f32[2,4,3,2,1,768]{5,1,4,3,2,0:T(4,128)S(1)} copy(f32[2,4,3,2,1,768]{5,4,3,2,1,0:T(1,128)} %get-tuple-element.167) | data formatting | bytes 294912
  32.5 0.7 copy.271
  33.2 0.7 copy.270
  35.1 0.6 subtract_reduce_fusion.12
  35.7 1.1 %fusion.27 = (f32[3,3,2,2,768]{4,3,2,0,1:T(2,128)S(1)}, f32[3,3,2,2,768]{4,3,2,0,1:T(2,128)S(1)}) fusion(f32[2,3,3,2,1,768]{5,4,3,2,1,0:T(1,128)} %collective-permute-done.3, f32[2,3,3,2,1,768]{5,4,3,2,1,0:T(1,128)S(1)} %copy-done.47), kind=kLoop, calls=%fused_computation.260 | loop fusion | flops 82944 | bytes 442368 | tf_op jit(solution)/shard_map/transpose | solution.py:63
  36.8 0.9 %fusion.25 = (f32[3,3,2,2,768]{4,3,2,0,1:T(2,128)S(1)}, f32[3,3,2,2,768]{4,3,2,0,1:T(2,128)S(1)}) fusion(f32[2,3,3,1,2,768]{5,4,3,2,1,0:T(2,128)} %collective-permute-done.5, f32[2,3,3,1,2,768]{5,4,3,2,1,0:T(2,128)S(1)} %copy-done.46), kind=kLoop, calls=%fused_computation.258 | loop fusion | flops 82944 | bytes 442368 | tf_op jit(solution)/shard_map/transpose | solution.py:63
  37.8 1.0 %broadcast_multiply_fusion = (f32[2,4,3,1,2,768]{5,1,4,3,2,0:T(4,128)S(1)}, f32[2,4,3,4,2,768]{5,1,4,3,2,0:T(4,128)S(1)}) fusion(f32[2,4,3,1,2,768]{5,1,4,3,2,0:T(4,128)} %collective-permute-done, f32[]{:T(128)S(6)} %select_n.8), kind=kLoop, calls=%fused_computation.311 | loop fusion | flops 36863 | bytes 442372 | tf_op jit(solution)/shard_map/mul | solution.py:152
  38.8 1.0 %broadcast_multiply_fusion.2 = (f32[2,4,3,1,2,768]{5,1,4,3,2,0:T(4,128)S(1)}, f32[2,4,3,4,2,768]{5,1,4,3,2,0:T(4,128)S(1)}) fusion(f32[2,4,3,1,2,768]{5,1,4,3,2,0:T(4,128)} %collective-permute-done.1, f32[]{:T(128)S(6)} %select_n.7, f32[2,4,3,4,2,768]{5,1,4,3,2,0:T(4,128)S(1)} %constant_dynamic-update-slice_fusion.1), kind=kLoop, calls=%fused_computation.313 | loop fusion | flops 36864 | bytes 442372 | tf_op jit(solution)/shard_map/mul | solution.py:151
  39.8 1.4 %fusion.124 = (f32[1,3,2,2,768]{4,0,3,2,1:T(1,128)S(1)}, f32[1,3,2,2,768]{4,0,3,2,1:T(1,128)S(1)}, f32[1,3,2,2,768]{4,0,3,2,1:T(1,128)S(1)}, f32[1,3,2,2,768]{4,...) fusion(f32[2,4,3,1,2,768]{5,1,4,3,2,0:T(4,128)S(1)} %get-tuple-, ...), kind=kLoop, calls=%fused_computation.470 | loop fusion | flops 73728 | bytes 589824 | tf_op jit(solution)/shard_map/stack;squeeze | solution.py:52
  41.5 1.0 %fusion.9 = f32[2,4,3,2,2,768]{5,1,4,3,2,0:T(4,128)S(1)} fusion(f32[2,4,3,1,2,768]{5,1,4,3,2,0:T(4,128)S(1)} %get-tuple-element.238, f32[2,4,3,1,2,768]{5,1,4,3,2,0:T(4,128)} %copy.476, f32[1,4,3,2,2,768]{5,1,4,3,2,0:T(4,128)S(1)} %maximum_bitcast_fusion.17, f32[1,4,3,2,2,768]{5,1,4,3,2,0:T(4,128)S(1)} %maximum_bitcast_fusion.16), kind=kLoop, calls=%fused_computation.166 | loop fusion | flops 294912 | bytes 884736 | tf_op jit(solution)/shard_map/add | solution.py:56
  42.7 2.3 %collective-permute-start.2 = (f32[2,4,3,4,1,768]{5,1,4,3,2,0:T(4,128)S(1)}, f32[2,4,3,4,1,768]{5,1,4,3,2,0:T(4,128)S(1)}, u32[]{:S(2)}, u32[]{:S(2)}) collective-permute-start(f32[2,4,3,4,1,768]{5,1,4,3,2,0:T(4,128)S(1)} %get-tuple-element.85), channel_id=1, source_target_pairs={{1,0},{2,1},{3,2},{0,3},{5,4},{6,5},{7,6},{4,7},{9,8},{10,9},{11,1... | collective-permute-start | bytes 884744 | tf_op jit(solution)/shard_map/ppermute | solution.py:28
  45.0 1.5 %fusion.132 = (f32[1,3,2,2,768]{4,0,3,2,1:T(1,128)S(1)}, f32[1,3,2,2,768]{4,0,3,2,1:T(1,128)S(1)}, f32[1,3,2,2,768]{4,0,3,2,1:T(1,128)S(1)}, f32[1,3,2,2,768]{4,...) fusion(f32[2,4,3,1,2,768]{5,1,4,3,2,0:T(4,128)} %copy.477, ...), kind=kLoop, calls=%fused_computation.478 | loop fusion | flops 73728 | bytes 589824 | tf_op jit(solution)/shard_map/stack;squeeze | solution.py:52
  46.8 1.0 %fusion.8 = f32[2,4,3,2,2,768]{5,1,4,3,2,0:T(4,128)S(1)} fusion(f32[2,4,3,1,2,768]{5,1,4,3,2,0:T(4,128)} %copy.477, f32[2,4,3,1,2,768]{5,1,4,3,2,0:T(4,128)S(1)} %get-tuple-element.236, f32[1,4,3,2,2,768]{5,1,4,3,2,0:T(4,128)S(1)} %get-tuple-element.253, f32[1,4,3,2,2,768]{5,1,4,3,2,0:T(4,128)S(1)} %get-tuple-element.252), kind=kLoop, calls=%fused_computation.165 | loop fusion | flops 221184 | bytes 884736 | tf_op jit(solution)/shard_map/add | solution.py:56
  48.2 4.2 %collective-permute-done.2 = f32[2,4,3,4,1,768]{5,1,4,3,2,0:T(4,128)S(1)} collective-permute-done((f32[2,4,3,4,1,768]{5,1,4,3,2,0:T(4,128)S(1)}, f32[2,4,3,4,1,768]{5,1,4,3,2,0:T(4,128)S(1)}, u32[]{:S(2)}, u32[]{:S(2)}) %collective-permute-start.2) | collective-permute-done | bytes 294944 | tf_op jit(solution)/shard_map/ppermute | solution.py:28
  52.7 7.5 %collective-permute-done.4 = f32[2,4,3,4,1,768]{5,1,4,3,2,0:T(4,128)S(1)} collective-permute-done((f32[2,4,3,4,1,768]{5,1,4,3,2,0:T(4,128)S(1)}, f32[2,4,3,4,1,768]{5,1,4,3,2,0:T(4,128)S(1)}, u32[]{:S(2)}, u32[]{:S(2)}) %collective-permute-start.4) | collective-permute-done | bytes 294944 | tf_op jit(solution)/shard_map/ppermute | solution.py:25
  62.1 0.7 subtract_reduce_fusion.9
  63.5 0.8 slice_bitcast_fusion.11
  65.1 0.7 fusion.160
  65.8 0.7 fusion.159
  68.1 0.7 slice_bitcast_fusion.9
  69.8 1.8 %collective-permute-start.6 = (f32[2,4,3,2,1,768]{5,1,4,3,2,0:T(4,128)S(1)}, f32[2,4,3,2,1,768]{5,1,4,3,2,0:T(4,128)S(1)}, u32[]{:S(2)}, u32[]{:S(2)}) collective-permute-start(f32[2,4,3,2,1,768]{5,1,4,3,2,0:T(4,128)S(1)} %copy-done.51), channel_id=1, source_target_pairs={{0,3},{1,0},{2,1},{3,2},{4,7},{5,4},{6,5},{7,6},{8,11},{9,8},{10,9... | collective-permute-start | bytes 442376 | tf_op jit(solution)/shard_map/ppermute | solution.py:36
  71.6 1.9 %collective-permute-start.7 = (f32[2,4,3,1,2,768]{5,1,4,3,2,0:T(4,128)S(1)}, f32[2,4,3,1,2,768]{5,1,4,3,2,0:T(4,128)S(1)}, u32[]{:S(2)}, u32[]{:S(2)}) collective-permute-start(f32[2,4,3,1,2,768]{5,1,4,3,2,0:T(4,128)S(1)} %copy-done.50), channel_id=1, source_target_pairs={{0,28},{4,0},{8,4},{12,8},{16,12},{20,16},{24,20},{28,24},{1,29},{... | collective-permute-start | bytes 442376 | tf_op jit(solution)/shard_map/ppermute | solution.py:36
  73.5 3.0 %add_reduce_fusion.7 = (f32[3,3,2,2,768]{4,3,2,1,0:T(2,128)S(1)}, f32[3,3,2,2,768]{4,3,2,1,0:T(2,128)S(1)}, f32[3,3,2,2,768]{4,3,2,1,0:T(2,128)S(1)}, f32[3,3,2,...) fusion(f32[4,3,2,2,768]{4,0,3,2,1:T(4,128)S(1)} %copy-done.40, ...), kind=kLoop, calls=%fused_computation.136 | loop fusion | flops 3317760 | bytes 2359296 | tf_op jit(solution)/shard_map/reduce_sum | solution.py:88
  78.8 3.0 %add_reduce_fusion.6 = (f32[3,3,2,2,768]{4,3,2,1,0:T(2,128)S(1)}, f32[3,3,2,2,768]{4,3,2,1,0:T(2,128)S(1)}, f32[3,3,2,2,768]{4,3,2,1,0:T(2,128)S(1)}, f32[3,3,2,...) fusion(f32[4,3,2,2,768]{4,0,3,2,1:T(4,128)S(1)} %copy-done.36, ...), kind=kLoop, calls=%fused_computation.134 | loop fusion | flops 3317760 | bytes 2359296 | tf_op jit(solution)/shard_map/reduce_sum | solution.py:88
  82.1 0.5 subtract_reduce_fusion.19
  86.1 1.3 %pad_maximum_fusion = f32[4,2,3,3,2,2,768]{6,5,4,3,2,1,0:T(2,128)} fusion(f32[1,2,3,3,2,2,768]{6,5,4,3,2,1,0:T(2,128)S(1)} %maximum_bitcast_fusion.3, f32[1,2,3,3,2,2,768]{6,5,4,3,2,1,0:T(2,128)S(1)} %maximum_bitcast_fusion.2, f32[1,2,3,3,2,2,768]{6,5,4,3,2,1,0:T(2,128)S(1)} %maximum_bitcast_fusion.1, f32[1,2,3,3,2,2,768]{6,5,4,3,2,1,0:T(2,128)S(1)} %maximum_bitcast_fusion), kind=kLoop, calls=%fused_computation | loop fusion | flops 663552 | bytes 1769472 | tf_op jit(solution)/shard_map/stack | solution.py:187
  (276 shorter events, 21.5 us)
Async XLA Ops:
  0.6 5.9 %copy-start.1 = (f32[4,2,3,3,2,2,768]{6,5,4,3,2,1,0:T(2,128)S(1)}, f32[4,2,3,3,2,2,768]{6,5,4,3,2,1,0:T(2,128)}, u32[]{:S(2)}) copy-start(f32[4,2,3,3,2,2,768]{6,5,4,3,2,1,0:T(2,128)} %param.4) | copy-start | bytes 2654212
  1.7 9.0 %copy-start = (f32[2,4,3,2,2,768]{5,4,3,2,1,0:T(2,128)S(1)}, f32[2,4,3,2,2,768]{5,4,3,2,1,0:T(2,128)}, u32[]{:S(2)}) copy-start(f32[2,4,3,2,2,768]{5,4,3,2,1,0:T(2,128)} %param.3) | copy-start | bytes 884740
  2.4 36.4 %collective-permute-start.1 = (f32[2,4,3,1,2,768]{5,1,4,3,2,0:T(4,128)}, f32[2,4,3,1,2,768]{5,1,4,3,2,0:T(4,128)}, u32[]{:S(2)}, u32[]{:S(2)}) collective-permute-start(f32[2,4,3,1,2,768]{5,1,4,3,2,0:T(4,128)} %copy.477), channel_id=1, source_target_pairs={{4,0},{8,4},{12,8},{16,12},{20,16},{24,20},{28,24},{0,28},{5,1},{9... | collective-permute-start | bytes 442376 | tf_op jit(solution)/shard_map/ppermute | solution.py:28
  6.5 31.3 %collective-permute-start = (f32[2,4,3,1,2,768]{5,1,4,3,2,0:T(4,128)}, f32[2,4,3,1,2,768]{5,1,4,3,2,0:T(4,128)}, u32[]{:S(2)}, u32[]{:S(2)}) collective-permute-start(f32[2,4,3,1,2,768]{5,1,4,3,2,0:T(4,128)} %copy.476), channel_id=1, source_target_pairs={{0,4},{4,8},{8,12},{12,16},{16,20},{20,24},{24,28},{28,0},{1,5},{5... | collective-permute-start | bytes 442376 | tf_op jit(solution)/shard_map/ppermute | solution.py:25
  8.4 27.3 %collective-permute-start.3 = (f32[2,3,3,2,1,768]{5,4,3,2,1,0:T(1,128)}, f32[2,3,3,2,1,768]{5,4,3,2,1,0:T(1,128)}, u32[]{:S(2)}, u32[]{:S(2)}) collective-permute-start(f32[2,3,3,2,1,768]{5,4,3,2,1,0:T(1,128)} %get-tuple-element.234), channel_id=1, source_target_pairs={{0,1},{1,2},{2,3},{3,0},{4,5},{5,6},{6,7},{7,4},{8,9},{9,10},{10,1... | collective-permute-start | bytes 331784 | tf_op jit(solution)/shard_map/ppermute | solution.py:36
  10.7 26.1 %collective-permute-start.5 = (f32[2,3,3,1,2,768]{5,4,3,2,1,0:T(2,128)}, f32[2,3,3,1,2,768]{5,4,3,2,1,0:T(2,128)}, u32[]{:S(2)}, u32[]{:S(2)}) collective-permute-start(f32[2,3,3,1,2,768]{5,4,3,2,1,0:T(2,128)} %get-tuple-element.230), channel_id=1, source_target_pairs={{0,4},{4,8},{8,12},{12,16},{16,20},{20,24},{24,28},{28,0},{1,5},{5... | collective-permute-start | bytes 331784 | tf_op jit(solution)/shard_map/ppermute | solution.py:36
  13.5 21.2 %copy-start.24 = (f32[3,3,2,2,768]{4,3,2,1,0:T(2,128)}, f32[3,3,2,2,768]{4,3,2,1,0:T(2,128)S(1)}, u32[]{:S(2)}) copy-start(f32[3,3,2,2,768]{4,3,2,1,0:T(2,128)S(1)} %get-tuple-element.69) | copy-start | bytes 331780
  14.2 1.6 %copy-start.3 = (f32[2,2,6,6,2,2,768]{6,5,4,3,2,1,0:T(2,128)S(1)}, f32[2,2,6,6,2,2,768]{6,5,4,3,2,1,0:T(2,128)}, u32[]{:S(2)}) copy-start(f32[2,2,6,6,2,2,768]{6,5,4,3,2,1,0:T(2,128)} %param.5) | copy-start | bytes 5308420
  20.0 1.7 %copy-start.2 = (f32[2,4,3,2,2,768]{5,4,3,2,1,0:T(2,128)S(1)}, f32[2,4,3,2,2,768]{5,4,3,2,1,0:T(2,128)}, u32[]{:S(2)}) copy-start(f32[2,4,3,2,2,768]{5,4,3,2,1,0:T(2,128)} %reshape.579) | copy-start | bytes 884740
  22.9 1.6 %copy-start.33 = (f32[1,2,3,3,2,2,768]{6,5,4,3,2,1,0:T(2,128)S(1)}, f32[1,2,3,3,2,2,768]{6,5,4,3,2,1,0:T(2,128)}, u32[]{:S(2)}) copy-start(f32[1,2,3,3,2,2,768]{6,5,4,3,2,1,0:T(2,128)} %get-tuple-element.65) | copy-start | bytes 663556
  29.3 5.4 %copy-start.10 = (f32[4,3,2,2,768]{4,0,3,2,1:T(4,128)}, f32[4,3,2,2,768]{4,0,3,2,1:T(4,128)S(1)}, u32[]{:S(2)}) copy-start(f32[4,3,2,2,768]{4,0,3,2,1:T(4,128)S(1)} %get-tuple-element.190) | copy-start | bytes 442372
  29.3 5.4 %copy-start.12 = (f32[4,3,2,2,768]{4,0,3,2,1:T(4,128)}, f32[4,3,2,2,768]{4,0,3,2,1:T(4,128)S(1)}, u32[]{:S(2)}) copy-start(f32[4,3,2,2,768]{4,0,3,2,1:T(4,128)S(1)} %get-tuple-element.191) | copy-start | bytes 442372
  30.6 1.9 %copy-start.45 = (f32[2,4,3,2,1,768]{5,4,3,2,1,0:T(1,128)S(1)}, f32[2,4,3,2,1,768]{5,4,3,2,1,0:T(1,128)}, u32[]{:S(2)}) copy-start(f32[2,4,3,2,1,768]{5,4,3,2,1,0:T(1,128)} %get-tuple-element.166) | copy-start | bytes 442372
  30.6 1.9 %copy-start.42 = (f32[4,3,2,2,768]{4,3,2,1,0:T(2,128)S(1)}, f32[4,3,2,2,768]{4,3,2,1,0:T(2,128)}, u32[]{:S(2)}) copy-start(f32[4,3,2,2,768]{4,3,2,1,0:T(2,128)} %get-tuple-element.123) | copy-start | bytes 442372
  30.6 2.6 %copy-start.41 = (f32[4,3,2,2,768]{4,3,2,1,0:T(2,128)S(1)}, f32[4,3,2,2,768]{4,3,2,1,0:T(2,128)}, u32[]{:S(2)}) copy-start(f32[4,3,2,2,768]{4,3,2,1,0:T(2,128)} %get-tuple-element.122) | copy-start | bytes 442372
  31.0 3.0 %copy-start.6 = (f32[4,3,2,2,768]{4,0,3,2,1:T(4,128)S(1)}, f32[4,3,2,2,768]{4,0,3,2,1:T(4,128)}, u32[]{:S(2)}) copy-start(f32[4,3,2,2,768]{4,0,3,2,1:T(4,128)} %get-tuple-element.210) | copy-start | bytes 442372
  31.0 3.0 %copy-start.8 = (f32[4,3,2,2,768]{4,0,3,2,1:T(4,128)S(1)}, f32[4,3,2,2,768]{4,0,3,2,1:T(4,128)}, u32[]{:S(2)}) copy-start(f32[4,3,2,2,768]{4,0,3,2,1:T(4,128)} %get-tuple-element.211) | copy-start | bytes 442372
  31.0 3.0 %copy-start.28 = (f32[3,3,2,2,768]{4,3,2,1,0:T(2,128)S(1)}, f32[3,3,2,2,768]{4,3,2,1,0:T(2,128)}, u32[]{:S(2)}) copy-start(f32[3,3,2,2,768]{4,3,2,1,0:T(2,128)} %get-tuple-element.71) | copy-start | bytes 331780
  31.0 3.0 %copy-start.30 = (f32[3,3,2,2,768]{4,3,2,1,0:T(2,128)S(1)}, f32[3,3,2,2,768]{4,3,2,1,0:T(2,128)}, u32[]{:S(2)}) copy-start(f32[3,3,2,2,768]{4,3,2,1,0:T(2,128)} %get-tuple-element.72) | copy-start | bytes 331780
  31.0 3.3 %copy-start.43 = (f32[4,3,2,2,768]{4,0,3,2,1:T(4,128)S(1)}, f32[4,3,2,2,768]{4,0,3,2,1:T(4,128)}, u32[]{:S(2)}) copy-start(f32[4,3,2,2,768]{4,0,3,2,1:T(4,128)} %get-tuple-element.200) | copy-start | bytes 442372
  31.0 3.3 %copy-start.44 = (f32[4,3,2,2,768]{4,0,3,2,1:T(4,128)S(1)}, f32[4,3,2,2,768]{4,0,3,2,1:T(4,128)}, u32[]{:S(2)}) copy-start(f32[4,3,2,2,768]{4,0,3,2,1:T(4,128)} %get-tuple-element.201) | copy-start | bytes 442372
  31.2 3.2 %copy-start.48 = (f32[3,3,2,2,768]{4,3,2,1,0:T(2,128)S(1)}, f32[3,3,2,2,768]{4,3,2,1,0:T(2,128)}, u32[]{:S(2)}) copy-start(f32[3,3,2,2,768]{4,3,2,1,0:T(2,128)} %squeeze.18) | copy-start | bytes 331780
  31.2 3.2 %copy-start.49 = (f32[3,3,2,2,768]{4,3,2,1,0:T(2,128)S(1)}, f32[3,3,2,2,768]{4,3,2,1,0:T(2,128)}, u32[]{:S(2)}) copy-start(f32[3,3,2,2,768]{4,3,2,1,0:T(2,128)} %neg.37) | copy-start | bytes 331780
  31.2 3.6 %copy-start.26 = (f32[3,3,2,2,768]{4,3,2,1,0:T(2,128)S(1)}, f32[3,3,2,2,768]{4,3,2,1,0:T(2,128)}, u32[]{:S(2)}) copy-start(f32[3,3,2,2,768]{4,3,2,1,0:T(2,128)} %get-tuple-element.70) | copy-start | bytes 331780
  33.2 2.5 %copy-start.47 = (f32[2,3,3,2,1,768]{5,4,3,2,1,0:T(1,128)S(1)}, f32[2,3,3,2,1,768]{5,4,3,2,1,0:T(1,128)}, u32[]{:S(2)}) copy-start(f32[2,3,3,2,1,768]{5,4,3,2,1,0:T(1,128)} %get-tuple-element.235) | copy-start | bytes 331780
  33.9 2.9 %copy-start.46 = (f32[2,3,3,1,2,768]{5,4,3,2,1,0:T(2,128)S(1)}, f32[2,3,3,1,2,768]{5,4,3,2,1,0:T(2,128)}, u32[]{:S(2)}) copy-start(f32[2,3,3,1,2,768]{5,4,3,2,1,0:T(2,128)} %get-tuple-element.231) | copy-start | bytes 331780
  42.7 9.7 %collective-permute-start.2 = (f32[2,4,3,4,1,768]{5,1,4,3,2,0:T(4,128)S(1)}, f32[2,4,3,4,1,768]{5,1,4,3,2,0:T(4,128)S(1)}, u32[]{:S(2)}, u32[]{:S(2)}) collective-permute-start(f32[2,4,3,4,1,768]{5,1,4,3,2,0:T(4,128)S(1)} %get-tuple-element.85), channel_id=1, source_target_pairs={{1,0},{2,1},{3,2},{0,3},{5,4},{6,5},{7,6},{4,7},{9,8},{10,9},{11,1... | collective-permute-start | bytes 884744 | tf_op jit(solution)/shard_map/ppermute | solution.py:28
  45.0 15.2 %collective-permute-start.4 = (f32[2,4,3,4,1,768]{5,1,4,3,2,0:T(4,128)S(1)}, f32[2,4,3,4,1,768]{5,1,4,3,2,0:T(4,128)S(1)}, u32[]{:S(2)}, u32[]{:S(2)}) collective-permute-start(f32[2,4,3,4,1,768]{5,1,4,3,2,0:T(4,128)S(1)} %get-tuple-element.84), channel_id=1, source_target_pairs={{0,1},{1,2},{2,3},{3,0},{4,5},{5,6},{6,7},{7,4},{8,9},{9,10},{10,1... | collective-permute-start | bytes 884744 | tf_op jit(solution)/shard_map/ppermute | solution.py:25
  61.0 1.8 %copy-start.4 = (f32[4,3,2,2,768]{4,0,3,2,1:T(4,128)}, f32[4,3,2,2,768]{4,0,3,2,1:T(4,128)S(1)}, u32[]{:S(2)}) copy-start(f32[4,3,2,2,768]{4,0,3,2,1:T(4,128)S(1)} %get-tuple-element.169) | copy-start | bytes 442372
  61.5 1.3 %copy-start.34 = (f32[1,4,3,2,2,768]{5,1,4,3,2,0:T(4,128)S(1)}, f32[1,4,3,2,2,768]{5,1,4,3,2,0:T(4,128)}, u32[]{:S(2)}) copy-start(f32[1,4,3,2,2,768]{5,1,4,3,2,0:T(4,128)} %copy.181) | copy-start | bytes 442372
  61.5 1.3 %copy-start.35 = (f32[1,4,3,2,2,768]{5,1,4,3,2,0:T(4,128)S(1)}, f32[1,4,3,2,2,768]{5,1,4,3,2,0:T(4,128)}, u32[]{:S(2)}) copy-start(f32[1,4,3,2,2,768]{5,1,4,3,2,0:T(4,128)} %copy.180) | copy-start | bytes 442372
  63.5 1.6 %copy-start.15 = (f32[2,4,3,2,2,768]{5,4,3,2,1,0:T(2,128)}, f32[2,4,3,2,2,768]{5,4,3,2,1,0:T(2,128)S(1)}, u32[]{:S(2)}) copy-start(f32[2,4,3,2,2,768]{5,4,3,2,1,0:T(2,128)S(1)} %copy.302) | copy-start | bytes 884740
  68.7 2.8 %copy-start.50 = (f32[2,4,3,1,2,768]{5,1,4,3,2,0:T(4,128)S(1)}, f32[2,4,3,1,2,768]{5,1,4,3,2,0:T(4,128)}, u32[]{:S(2)}) copy-start(f32[2,4,3,1,2,768]{5,1,4,3,2,0:T(4,128)} %get-tuple-element.97) | copy-start | bytes 442372
  68.7 4.7 %copy-start.5 = (f32[4,3,2,2,768]{4,0,3,2,1:T(4,128)S(1)}, f32[4,3,2,2,768]{4,0,3,2,1:T(4,128)}, u32[]{:S(2)}) copy-start(f32[4,3,2,2,768]{4,0,3,2,1:T(4,128)} %copy-done.4) | copy-start | bytes 442372
  68.7 4.7 %copy-start.7 = (f32[4,3,2,2,768]{4,0,3,2,1:T(4,128)S(1)}, f32[4,3,2,2,768]{4,0,3,2,1:T(4,128)}, u32[]{:S(2)}) copy-start(f32[4,3,2,2,768]{4,0,3,2,1:T(4,128)} %get-tuple-element.210) | copy-start | bytes 442372
  68.7 4.7 %copy-start.9 = (f32[4,3,2,2,768]{4,0,3,2,1:T(4,128)S(1)}, f32[4,3,2,2,768]{4,0,3,2,1:T(4,128)}, u32[]{:S(2)}) copy-start(f32[4,3,2,2,768]{4,0,3,2,1:T(4,128)} %get-tuple-element.211) | copy-start | bytes 442372
  68.8 4.7 %copy-start.11 = (f32[4,3,2,2,768]{4,0,3,2,1:T(4,128)S(1)}, f32[4,3,2,2,768]{4,0,3,2,1:T(4,128)}, u32[]{:S(2)}) copy-start(f32[4,3,2,2,768]{4,0,3,2,1:T(4,128)} %copy-done.10) | copy-start | bytes 442372
  68.8 4.7 %copy-start.13 = (f32[4,3,2,2,768]{4,0,3,2,1:T(4,128)S(1)}, f32[4,3,2,2,768]{4,0,3,2,1:T(4,128)}, u32[]{:S(2)}) copy-start(f32[4,3,2,2,768]{4,0,3,2,1:T(4,128)} %copy-done.12) | copy-start | bytes 442372
  68.9 4.5 %copy-start.39 = (f32[4,3,2,2,768]{4,0,3,2,1:T(4,128)S(1)}, f32[4,3,2,2,768]{4,0,3,2,1:T(4,128)}, u32[]{:S(2)}) copy-start(f32[4,3,2,2,768]{4,0,3,2,1:T(4,128)} %get-tuple-element.134) | copy-start | bytes 442372
  68.9 4.5 %copy-start.40 = (f32[4,3,2,2,768]{4,0,3,2,1:T(4,128)S(1)}, f32[4,3,2,2,768]{4,0,3,2,1:T(4,128)}, u32[]{:S(2)}) copy-start(f32[4,3,2,2,768]{4,0,3,2,1:T(4,128)} %get-tuple-element.135) | copy-start | bytes 442372
  69.8 7.2 %collective-permute-start.6 = (f32[2,4,3,2,1,768]{5,1,4,3,2,0:T(4,128)S(1)}, f32[2,4,3,2,1,768]{5,1,4,3,2,0:T(4,128)S(1)}, u32[]{:S(2)}, u32[]{:S(2)}) collective-permute-start(f32[2,4,3,2,1,768]{5,1,4,3,2,0:T(4,128)S(1)} %copy-done.51), channel_id=1, source_target_pairs={{0,3},{1,0},{2,1},{3,2},{4,7},{5,4},{6,5},{7,6},{8,11},{9,8},{10,9... | collective-permute-start | bytes 442376 | tf_op jit(solution)/shard_map/ppermute | solution.py:36
  71.6 6.2 %collective-permute-start.7 = (f32[2,4,3,1,2,768]{5,1,4,3,2,0:T(4,128)S(1)}, f32[2,4,3,1,2,768]{5,1,4,3,2,0:T(4,128)S(1)}, u32[]{:S(2)}, u32[]{:S(2)}) collective-permute-start(f32[2,4,3,1,2,768]{5,1,4,3,2,0:T(4,128)S(1)} %copy-done.50), channel_id=1, source_target_pairs={{0,28},{4,0},{8,4},{12,8},{16,12},{20,16},{24,20},{28,24},{1,29},{... | collective-permute-start | bytes 442376 | tf_op jit(solution)/shard_map/ppermute | solution.py:36
  78.6 3.5 %copy-start.29 = (f32[3,3,2,2,768]{4,3,2,1,0:T(2,128)S(1)}, f32[3,3,2,2,768]{4,3,2,1,0:T(2,128)}, u32[]{:S(2)}) copy-start(f32[3,3,2,2,768]{4,3,2,1,0:T(2,128)} %get-tuple-element.71) | copy-start | bytes 331780
  78.6 3.5 %copy-start.31 = (f32[3,3,2,2,768]{4,3,2,1,0:T(2,128)S(1)}, f32[3,3,2,2,768]{4,3,2,1,0:T(2,128)}, u32[]{:S(2)}) copy-start(f32[3,3,2,2,768]{4,3,2,1,0:T(2,128)} %get-tuple-element.72) | copy-start | bytes 331780
  82.1 1.7 %copy-start.21 = (f32[3,3,2,2,768]{4,3,2,1,0:T(2,128)S(1)}, f32[3,3,2,2,768]{4,3,2,1,0:T(2,128)}, u32[]{:S(2)}) copy-start(f32[3,3,2,2,768]{4,3,2,1,0:T(2,128)} %get-tuple-element.67) | copy-start | bytes 331780
  82.1 1.7 %copy-start.23 = (f32[3,3,2,2,768]{4,3,2,1,0:T(2,128)S(1)}, f32[3,3,2,2,768]{4,3,2,1,0:T(2,128)}, u32[]{:S(2)}) copy-start(f32[3,3,2,2,768]{4,3,2,1,0:T(2,128)} %get-tuple-element.68) | copy-start | bytes 331780
  83.0 1.7 %copy-start.17 = (f32[3,3,2,2,768]{4,3,2,1,0:T(2,128)S(1)}, f32[3,3,2,2,768]{4,3,2,1,0:T(2,128)}, u32[]{:S(2)}) copy-start(f32[3,3,2,2,768]{4,3,2,1,0:T(2,128)} %get-tuple-element.66) | copy-start | bytes 331780
  83.0 1.7 %copy-start.19 = (f32[3,3,2,2,768]{4,3,2,1,0:T(2,128)S(1)}, f32[3,3,2,2,768]{4,3,2,1,0:T(2,128)}, u32[]{:S(2)}) copy-start(f32[3,3,2,2,768]{4,3,2,1,0:T(2,128)} %get-tuple-element.73) | copy-start | bytes 331780
  (12 other events, 12.1 us)
where the time goes:
time: 88.1 us; the launch traced here: 87.4 us
  other arithmetic  34.7 us (39%)
  local copies, waits for them, and re-layouts  27.7 us (31%)
  waiting for transfers between devices  11.7 us (13%)
  starting transfers between devices  10.9 us (12%)
  between operations  2.44 us (3%)
    ppermute x2, waiting for transfers between devices, with_halo(): lax.ppermute(lax.slice_in_dim(block, block.shape[dim] - width, None, axis...  7.47 us
    another operation x28, other arithmetic, apply_gamma(): return jnp.stack([jnp.stack(parts_re), jnp.stack(parts_im)])  7.12 us
    reduce_sum x2, other arithmetic, spin_outer(): out_re = jnp.sum(left_re * right_re + left_im * right_im, axis=0)  6.07 us
    ppermute x2, starting transfers between devices, with_halo(): lax.ppermute(lax.slice_in_dim(block, 0, width, axis=dim), axis, backward)  5.66 us
    unnamed x158, local copies, waits for them, and re-layouts  5.64 us
    ppermute x4, starting transfers between devices, passed_along(): return lax.ppermute(value, axis, pairs)  5.25 us
    ppermute x2, waiting for transfers between devices, with_halo(): lax.ppermute(lax.slice_in_dim(block, 0, width, axis=dim), axis, backward)  4.25 us
    mul x8, local copies, waits for them, and re-layouts, spin_outer(): out_re = jnp.sum(left_re * right_re + left_im * right_im, axis=0)  3.83 us
  transfers between devices with their start and end apart: 8, of which 2 were waited for; matrix products, arithmetic and copies ran while one was open for 43% of the time, Pallas kernels for 0%

commit v1 on v0

v1 whole, which is shorter than its diff:
```python
import jax
import jax.numpy as jnp
from jax import lax
from jax.experimental import pallas as pl
from jax.experimental.pallas import tpu as pltpu
from jax.sharding import PartitionSpec as P

NX = 64
LANES = 128
TILE = 8
MESH = pl.DeviceIdType.MESH

bare_mass = -0.25
gamma_table = (
    ((3, 0.0, -1.0), (2, 0.0, -1.0), (1, 0.0, 1.0), (0, 0.0, 1.0)),
    ((3, -1.0, 0.0), (2, 1.0, 0.0), (1, 1.0, 0.0), (0, -1.0, 0.0)),
    ((2, 0.0, -1.0), (3, 0.0, 1.0), (0, 0.0, 1.0), (1, 0.0, -1.0)),
    ((2, 1.0, 0.0), (3, 1.0, 0.0), (0, 1.0, 0.0), (1, 1.0, 0.0)),
)


def add_signed(a, b, positive):
    return a + b if positive else a - b


def add_phase(a, b, phase_re, phase_im):
    if phase_im == 0.0:
        up = phase_re > 0
        return (add_signed(a[0], b[0], up), add_signed(a[1], b[1], up))
    up = phase_im > 0
    return (add_signed(a[0], b[1], not up), add_signed(a[1], b[0], up))


def half(mu, field, sign):
    out = []
    for s in range(2):
        source, p_re, p_im = gamma_table[mu][s]
        out.append(
            [add_phase(field[s][c], field[source][c], sign * p_re, sign * p_im) for c in range(3)]
        )
    return out


def add_whole(mu, total, halves, sign):
    out = [[add_phase(total[s][c], halves[s][c], 1.0, 0.0) for c in range(3)] for s in range(2)]
    for s in (2, 3):
        source, p_re, p_im = gamma_table[mu][s]
        out.append(
            [add_phase(total[s][c], halves[source][c], sign * p_re, sign * p_im) for c in range(3)]
        )
    return out


def csum(terms):
    total = terms[0]
    for term in terms[1:]:
        total = total + term
    return total


def mat_vec(link, vec, dagger):
    out = []
    for s in range(2):
        rows = []
        for a in range(3):
            re, im = [], []
            for b in range(3):
                h = vec[s][b]
                if dagger:
                    m = link[b][a]
                    re.append(m[0] * h[0] + m[1] * h[1])
                    im.append(m[0] * h[1] - m[1] * h[0])
                else:
                    m = link[a][b]
                    re.append(m[0] * h[0] - m[1] * h[1])
                    im.append(m[0] * h[1] + m[1] * h[0])
            rows.append((csum(re), csum(im)))
        out.append(rows)
    return out


def kernel(nt, nz, x_hbm, u_hbm, c_hbm, out_ref, force_ref, psi, link, clov, hm, hp, bl, sh_hm,
           sh_bl, prod, acc, hphi, sh_hphi, face_out, face_in, in_sem, send_sem, recv_sem):
    rows = psi.shape[1]
    face_t = rows // nt
    face_z = rows // nz
    chunks = rows // TILE
    t_place, z_place = lax.axis_index("ta"), lax.axis_index("gz")
    t_count, z_count = lax.axis_size("ta"), lax.axis_size("gz")
    t_next = (lax.rem(t_place + 1, t_count), z_place)
    t_prev = (lax.rem(t_place + t_count - 1, t_count), z_place)
    z_next = (t_place, lax.rem(z_place + 1, z_count))
    z_prev = (t_place, lax.rem(z_place + z_count - 1, z_count))
    low_sign = jnp.where(t_place == 0, -1.0, 1.0).astype(jnp.float32)
    high_sign = jnp.where(t_place == t_count - 1, -1.0, 1.0).astype(jnp.float32)

    barrier = pltpu.get_barrier_semaphore()
    for target in (t_next, t_prev, z_next, z_prev):
        pl.semaphore_signal(barrier, inc=1, device_id=target, device_id_type=MESH)

    loads = [pltpu.make_async_copy(x_hbm, psi, in_sem.at[0])]
    for mu in range(4):
        part = pl.ds(18 * mu, 18)
        loads.append(pltpu.make_async_copy(u_hbm.at[part], link.at[part], in_sem.at[1 + mu]))
    loads.append(pltpu.make_async_copy(c_hbm, clov, in_sem.at[5]))
    for n in (0, 4, 3, 1, 2, 5):
        loads[n].start()

    def window(v):
        return pl.ds(pl.multiple_of(v * TILE, TILE), TILE)

    def load_spinor(ref, at):
        return [[(ref[3 * s + c, at, :], ref[12 + 3 * s + c, at, :]) for c in range(3)] for s in range(4)]

    def load_half(ref, mu, at):
        return [[(ref[mu, 3 * s + c, at, :], ref[mu, 6 + 3 * s + c, at, :]) for c in range(3)] for s in range(2)]

    def store_half(ref, mu, at, value):
        for s in range(2):
            for c in range(3):
                ref[mu, 3 * s + c, at, :] = value[s][c][0]
                ref[mu, 6 + 3 * s + c, at, :] = value[s][c][1]

    def load_link(mu, at):
        return [[(link[18 * mu + 3 * a + b, at, :], link[18 * mu + 9 + 3 * a + b, at, :]) for b in range(3)] for a in range(3)]

    lane = lax.broadcasted_iota(jnp.int32, (rows, LANES), 1)
    row = lax.broadcasted_iota(jnp.int32, (rows, LANES), 0)
    lane_in = lax.rem(lane, NX)
    row_in = lax.rem(row, face_t)
    upper = lane >= NX

    def shift_x1(value, step):
        if step == 1:
            near, far = pltpu.roll(value, LANES - 1, 1), pltpu.roll(value, NX - 1, 1)
            return jnp.where(lane_in == NX - 1, far, near)
        near, far = pltpu.roll(value, 1, 1), pltpu.roll(value, LANES - NX + 1, 1)
        return jnp.where(lane_in == 0, far, near)

    def shift_x2(value, step):
        turned = pltpu.roll(value, NX, 1)
        if step == 1:
            near = pltpu.roll(turned, rows - nz, 0)
            far = pltpu.roll(turned, face_t - nz, 0)
            moved = jnp.where(row_in >= face_t - nz, far, near)
            return jnp.where(upper, moved, turned)
        near = pltpu.roll(turned, nz, 0)
        far = pltpu.roll(turned, rows - face_t + nz, 0)
        moved = jnp.where(row_in < nz, far, near)
        return jnp.where(upper, turned, moved)

    def z_ahead(src, dst, c):
        for z in range(nz - 1):
            dst[2, c, pl.ds(z, face_z, nz), :] = src[2, c, pl.ds(z + 1, face_z, nz), :]

    def z_behind(src, dst, c):
        for z in range(1, nz):
            dst[2, c, pl.ds(z, face_z, nz), :] = src[2, c, pl.ds(z - 1, face_z, nz), :]

    def t_ahead(src, dst, c):
        dst[3, c, pl.ds(0, rows - face_t), :] = src[3, c, pl.ds(face_t, rows - face_t), :]

    def t_behind(src, dst, c):
        dst[3, c, pl.ds(face_t, rows - face_t), :] = src[3, c, pl.ds(0, rows - face_t), :]

    def for_each(count, body):
        def step(i, carry):
            body(i)
            return carry

        lax.fori_loop(0, count, step, 0)

    targets = (t_prev, t_next, z_prev, z_next, t_prev, z_prev)
    sends = [
        pltpu.make_async_remote_copy(
            src_ref=face_out.at[k], dst_ref=face_in.at[k], send_sem=send_sem.at[k],
            recv_sem=recv_sem.at[k], device_id=targets[k], device_id_type=MESH,
        )
        for k in range(6)
    ]

    def project(mu, v):
        at = window(v)
        field = load_spinor(psi, at)
        store_half(hm, mu, at, half(mu, field, -1.0))
        ahead = half(mu, field, 1.0)
        store_half(hp, mu, at, ahead)
        store_half(bl, mu, at, mat_vec(load_link(mu, at), ahead, True))

    loads[0].wait()
    loads[4].wait()
    for_each(chunks, lambda v: project(3, v))

    for c in range(12):
        face_out[0, c, 0:face_t, :] = hm[3, c, 0:face_t, :]
        face_out[1, c, 0:face_t, :] = bl[3, c, rows - face_t:rows, :]
    pl.semaphore_wait(barrier, 4)
    sends[0].start()
    sends[1].start()
    loads[3].wait()
    for_each(chunks, lambda v: project(2, v))
    for c in range(12):
        face_out[2, c, 0:face_z, :] = hm[2, c, pl.ds(0, face_z, nz), :]
        face_out[3, c, 0:face_z, :] = bl[2, c, pl.ds(nz - 1, face_z, nz), :]
    sends[2].start()
    sends[3].start()

    loads[1].wait()
    for_each(chunks, lambda v: project(0, v))
    loads[2].wait()
    for_each(chunks, lambda v: project(1, v))

    def shifts(c):
        sh_hm[0, c] = shift_x1(hm[0, c], 1)
        sh_bl[0, c] = shift_x1(bl[0, c], -1)
        sh_hm[1, c] = shift_x2(hm[1, c], 1)
        sh_bl[1, c] = shift_x2(bl[1, c], -1)
        z_ahead(hm, sh_hm, c)
        z_behind(bl, sh_bl, c)
        t_ahead(hm, sh_hm, c)
        t_behind(bl, sh_bl, c)

    for_each(12, shifts)

    def hop(mu, at, total):
        ahead = mat_vec(load_link(mu, at), load_half(sh_hm, mu, at), False)
        store_half(prod, mu, at, ahead)
        total = add_whole(mu, total, ahead, -1.0)
        return add_whole(mu, total, load_half(sh_bl, mu, at), 1.0)

    zero = jnp.zeros((TILE, LANES), jnp.float32)

    loads[5].wait()

    def local(v):
        at = window(v)
        field = load_spinor(psi, at)
        total = [[(zero, zero)] * 3 for _ in range(4)]
        for mu in (0, 1):
            total = hop(mu, at, total)
        for s in range(4):
            for c in range(3):
                base = 36 * (s // 2) + 6 * (3 * (s % 2) + c)
                re = (4.0 + bare_mass) * field[s][c][0] - 0.5 * total[s][c][0]
                im = (4.0 + bare_mass) * field[s][c][1] - 0.5 * total[s][c][1]
                for k in range(6):
                    other = field[2 * (s // 2) + k // 3][k % 3]
                    c_re = clov[base + k, at, :]
                    c_im = clov[72 + base + k, at, :]
                    re = re + (c_re * other[0] - c_im * other[1])
                    im = im + (c_re * other[1] + c_im * other[0])
                acc[3 * s + c, at, :] = re
                acc[12 + 3 * s + c, at, :] = im

    for_each(chunks, local)

    for k in range(4):
        sends[k].wait_recv()

    for c in range(12):
        sh_hm[3, c, pl.ds(rows - face_t, face_t), :] = face_in[0, c, 0:face_t, :] * high_sign
        sh_bl[3, c, pl.ds(0, face_t), :] = face_in[1, c, 0:face_t, :] * low_sign
        sh_hm[2, c, pl.ds(nz - 1, face_z, nz), :] = face_in[2, c, 0:face_z, :]
        sh_bl[2, c, pl.ds(0, face_z, nz), :] = face_in[3, c, 0:face_z, :]

    def finish(v):
        at = window(v)
        total = [[(zero, zero)] * 3 for _ in range(4)]
        for mu in (2, 3):
            total = hop(mu, at, total)
        held = load_spinor(acc, at)
        phi = [
            [(held[s][c][0] - 0.5 * total[s][c][0], held[s][c][1] - 0.5 * total[s][c][1]) for c in range(3)]
            for s in range(4)
        ]
        for s in range(4):
            for c in range(3):
                out_ref[3 * s + c, at, :] = phi[s][c][0]
                out_ref[12 + 3 * s + c, at, :] = phi[s][c][1]
        for mu in range(4):
            store_half(hphi, mu, at, half(mu, phi, 1.0))

    for_each(chunks, finish)

    for c in range(12):
        face_out[4, c, 0:face_t, :] = hphi[3, c, 0:face_t, :]
        face_out[5, c, 0:face_z, :] = hphi[2, c, pl.ds(0, face_z, nz), :]
    sends[4].start()
    sends[5].start()

    def shifts_phi(c):
        sh_hphi[0, c] = shift_x1(hphi[0, c], 1)
        sh_hphi[1, c] = shift_x2(hphi[1, c], 1)
        z_ahead(hphi, sh_hphi, c)
        t_ahead(hphi, sh_hphi, c)

    for_each(12, shifts_phi)

    def force(mu, v):
        at = window(v)
        second = mat_vec(load_link(mu, at), load_half(sh_hphi, mu, at), False)
        second_right = load_half(hp, mu, at)
        first = load_half(prod, mu, at)
        first_right = half(mu, load_spinor(out_ref, at), -1.0)
        pairs = [(first[s], first_right[s]) for s in range(2)] + [(second[s], second_right[s]) for s in range(2)]

        def w_re(a, b):
            return csum([l[a][0] * r[b][0] + l[a][1] * r[b][1] for l, r in pairs])

        def w_im(a, b):
            return csum([l[a][1] * r[b][0] - l[a][0] * r[b][1] for l, r in pairs])

        diag = [w_im(a, a) for a in range(3)]
        third = (diag[0] + diag[1] + diag[2]) * (1.0 / 3.0)
        base = 18 * mu
        for a in range(3):
            force_ref[base + 4 * a, at, :] = zero
            force_ref[base + 9 + 4 * a, at, :] = diag[a] - third
            for b in range(a + 1, 3):
                re = 0.5 * (w_re(a, b) - w_re(b, a))
                im = 0.5 * (w_im(a, b) + w_im(b, a))
                force_ref[base + 3 * a + b, at, :] = re
                force_ref[base + 3 * b + a, at, :] = -re
                force_ref[base + 9 + 3 * a + b, at, :] = im
                force_ref[base + 9 + 3 * b + a, at, :] = im

    for_each(chunks, lambda v: force(0, v))
    for_each(chunks, lambda v: force(1, v))

    for k in (4, 5):
        sends[k].wait_recv()
    for c in range(12):
        sh_hphi[3, c, pl.ds(rows - face_t, face_t), :] = face_in[4, c, 0:face_t, :] * high_sign
        sh_hphi[2, c, pl.ds(nz - 1, face_z, nz), :] = face_in[5, c, 0:face_z, :]
    for_each(chunks, lambda v: force(2, v))
    for_each(chunks, lambda v: force(3, v))
    for k in range(6):
        sends[k].wait_send()


def to_rows(array):
    nt, nz, plane = array.shape[-3:]
    parts = plane // LANES
    grid = array.reshape((-1, nt, nz, parts, LANES))
    return jnp.swapaxes(grid, 2, 3).reshape((-1, nt * parts * nz, LANES))


def from_rows(rows, shape):
    nt, nz, plane = shape[-3:]
    grid = rows.reshape((-1, nt, plane // LANES, nz, LANES))
    return jnp.swapaxes(grid, 2, 3).reshape(shape)


def body(spinor, links, clover):
    nt, nz = spinor.shape[3], spinor.shape[4]
    x, u, c = to_rows(spinor), to_rows(links), to_rows(clover)
    rows = x.shape[1]
    face = max(rows // nt, rows // nz)

    def halves():
        return pltpu.VMEM((4, 12, rows, LANES), jnp.float32)

    applied, force = pl.pallas_call(
        lambda *refs: kernel(nt, nz, *refs),
        name="wilson",
        out_shape=(
            jax.ShapeDtypeStruct(x.shape, jnp.float32),
            jax.ShapeDtypeStruct(u.shape, jnp.float32),
        ),
        in_specs=[pl.BlockSpec(memory_space=pl.ANY)] * 3,
        out_specs=(pl.BlockSpec(memory_space=pltpu.VMEM),) * 2,
        scratch_shapes=[
            pltpu.VMEM(x.shape, jnp.float32),
            pltpu.VMEM(u.shape, jnp.float32),
            pltpu.VMEM(c.shape, jnp.float32),
            halves(), halves(), halves(), halves(), halves(), halves(),
            pltpu.VMEM(x.shape, jnp.float32),
            halves(), halves(),
            pltpu.VMEM((6, 12, face, LANES), jnp.float32),
            pltpu.VMEM((6, 12, face, LANES), jnp.float32),
            pltpu.SemaphoreType.DMA((6,)),
            pltpu.SemaphoreType.DMA((6,)),
            pltpu.SemaphoreType.DMA((6,)),
        ],
        compiler_params=pltpu.CompilerParams(collective_id=0, has_side_effects=True),
    )(x, u, c)
    return from_rows(applied, spinor.shape), from_rows(force, links.shape)


def solution(mesh):
    return jax.shard_map(
        body,
        mesh=mesh,
        in_specs=(
            P(None, None, None, "ta", "gz", None),
            P(None, None, None, None, "ta", "gz", None),
            P(None, None, None, None, "ta", "gz", None),
        ),
        out_specs=(
            P(None, None, None, "ta", "gz", None),
            P(None, None, None, None, "ta", "gz", None),
        ),
        check_vma=False,
    )
```

time: 88.1 us -> 28.3 us (0.32)
  the two profiles are of different devices: /device:TPU:0 before, /device:TPU:1 now
where the time goes in v1:
time: 28.3 us; the launch traced here: 28.2 us
  Pallas kernels  15.8 us (56%)
  local copies, waits for them, and re-layouts  11.7 us (41%)
  between operations  0.68 us (2%)
    pallas_call x1, Pallas kernels, body(): pl.pallas_call(lambda *refs: kernel(nt, nz, *refs), name='wilson', out_sh...  15.8 us
    transpose x3, local copies, waits for them, and re-layouts, to_rows(): return jnp.swapaxes(grid, 2, 3).reshape((-1, nt * parts * nz, LANES))  4.39 us
    reshape x3, local copies, waits for them, and re-layouts, to_rows(): grid = array.reshape((-1, nt, nz, parts, LANES))  3.59 us
    reshape x2, local copies, waits for them, and re-layouts, from_rows(): return jnp.swapaxes(grid, 2, 3).reshape(shape)  2.3 us
    reshape x2, local copies, waits for them, and re-layouts, from_rows(): grid = rows.reshape((-1, nt, plane // LANES, nz, LANES))  1.42 us

profile of v1, /device:TPU:1, one launch (start us, length us, event | category | flops | bytes accessed | tf_op | source)
XLA Modules:
  0.0 28.2 jit_solution(4380425639641552648)
XLA Ops:
  0.6 2.6 %reshape.38 = f32[144,2,2,6,128]{4,3,2,1,0:T(8,128)S(1)} reshape(f32[2,2,6,6,2,2,768]{6,5,4,3,2,1,0:T(2,128)} %param.5) | data formatting | bytes 3538944 | tf_op jit(solution)/shard_map/reshape | solution.py:344
  3.3 0.0 copy-start
  3.3 2.2 %copy.12 = f32[144,2,6,2,128]{4,3,2,1,0:T(2,128)} copy(f32[144,2,6,2,128]{4,2,3,1,0:T(8,128)S(1)} %bitcast.14) | data formatting | bytes 3538944 | tf_op jit(solution)/shard_map/transpose | solution.py:345
  5.5 0.0 copy-done
  5.5 0.0 copy-start.1
  5.5 0.7 %reshape.36 = f32[72,2,2,6,128]{4,3,2,1,0:T(8,128)S(1)} reshape(f32[4,2,3,3,2,2,768]{6,5,4,3,2,1,0:T(2,128)S(1)} %copy-done) | data formatting | bytes 1769472 | tf_op jit(solution)/shard_map/reshape | solution.py:344
  6.2 1.4 %copy.11 = f32[72,2,6,2,128]{4,3,2,1,0:T(2,128)} copy(f32[72,2,6,2,128]{4,2,3,1,0:T(8,128)S(1)} %bitcast.17) | data formatting | bytes 1769472 | tf_op jit(solution)/shard_map/transpose | solution.py:345
  7.5 0.0 copy-done.1
  7.5 0.2 reshape.34
  7.8 0.9 %copy.10 = f32[24,2,6,2,128]{4,3,2,1,0:T(2,128)} copy(f32[24,2,6,2,128]{4,2,3,1,0:T(8,128)S(1)} %bitcast.20) | data formatting | bytes 589824 | tf_op jit(solution)/shard_map/transpose | solution.py:345
  8.6 15.8 %wilson.1 = (f32[24,24,128]{2,1,0:T(8,128)}, f32[72,24,128]{2,1,0:T(8,128)}) custom-call(f32[24,24,128]{2,1,0:T(8,128)} %bitcast.21, f32[72,24,128]{2,1,0:T(8,128)} %bitcast.18, f32[144,24,128]{2,1,0:T(8,128)} %bitcast.15), custom_call_target="tpu_custom_call" | custom-call | tf_op jit(solution)/shard_map/wilson/pallas_call | solution.py:363
  24.4 0.0 copy-start.2
  24.4 1.4 %copy.17 = f32[72,2,6,2,128]{4,2,3,1,0:T(8,128)S(1)} copy(f32[72,2,6,2,128]{4,3,2,1,0:T(2,128)} %bitcast.22) | data formatting | bytes 1769472 | tf_op jit(solution)/shard_map/reshape | solution.py:350
  25.8 1.4 %reshape.43 = f32[4,2,3,3,2,2,768]{6,5,4,3,2,1,0:T(2,128)} reshape(f32[72,2,2,6,128]{4,3,2,1,0:T(8,128)S(1)} %bitcast.16) | data formatting | bytes 1769472 | tf_op jit(solution)/shard_map/reshape | solution.py:351
  27.2 0.0 copy-done.2
  27.2 0.1 copy.18
  27.3 0.9 %reshape.41 = f32[2,4,3,2,2,768]{5,4,3,2,1,0:T(2,128)} reshape(f32[24,2,2,6,128]{4,3,2,1,0:T(8,128)S(1)} %bitcast.19) | data formatting | bytes 589824 | tf_op jit(solution)/shard_map/reshape | solution.py:351
Async XLA Ops:
  3.3 2.2 %copy-start = (f32[4,2,3,3,2,2,768]{6,5,4,3,2,1,0:T(2,128)S(1)}, f32[4,2,3,3,2,2,768]{6,5,4,3,2,1,0:T(2,128)}, u32[]{:S(2)}) copy-start(f32[4,2,3,3,2,2,768]{6,5,4,3,2,1,0:T(2,128)} %param.4) | copy-start | bytes 2654212
  5.5 2.1 %copy-start.1 = (f32[2,4,3,2,2,768]{5,4,3,2,1,0:T(2,128)S(1)}, f32[2,4,3,2,2,768]{5,4,3,2,1,0:T(2,128)}, u32[]{:S(2)}) copy-start(f32[2,4,3,2,2,768]{5,4,3,2,1,0:T(2,128)} %param.3) | copy-start | bytes 884740
  24.4 2.8 %copy-start.2 = (f32[24,24,128]{2,1,0:T(8,128)S(1)}, f32[24,24,128]{2,1,0:T(8,128)}, u32[]{:S(2)}) copy-start(f32[24,24,128]{2,1,0:T(8,128)} %get-tuple-element.4) | copy-start | bytes 884740

commit v2 on v1

--- a/solution.py
+++ b/solution.py
@@ -79,8 +79,20 @@
     return out
 
 
-def kernel(nt, nz, x_hbm, u_hbm, c_hbm, out_ref, force_ref, psi, link, clov, hm, hp, bl, sh_hm,
-           sh_bl, prod, acc, hphi, sh_hphi, face_out, face_in, in_sem, send_sem, recv_sem):
+def flat(ref):
+    return ref.reshape(ref.shape[0], ref.shape[1] * ref.shape[2], ref.shape[3])
+
+
+def parts_of(whole, held):
+    parts = whole.shape[-1] // LANES
+    for t in range(whole.shape[-3]):
+        for q in range(parts):
+            yield whole.at[:, t, :, pl.ds(LANES * q, LANES)], held.at[:, parts * t + q]
+
+
+def kernel(nt, nz, x_hbm, u_hbm, c_hbm, out_hbm, force_hbm, psi_in, link_in, clov_in, phi_out, force_out, hm, hp, bl,
+           sh_hm, sh_bl, prod, acc, hphi, sh_hphi, face_out, face_in, in_sem, out_sem, send_sem, recv_sem):
+    psi, link, clov, out_ref, force_ref = map(flat, (psi_in, link_in, clov_in, phi_out, force_out))
     rows = psi.shape[1]
     face_t = rows // nt
     face_z = rows // nz
@@ -98,13 +110,31 @@
     for target in (t_next, t_prev, z_next, z_prev):
         pl.semaphore_signal(barrier, inc=1, device_id=target, device_id_type=MESH)
 
-    loads = [pltpu.make_async_copy(x_hbm, psi, in_sem.at[0])]
+    groups = [(x_hbm, psi_in)]
     for mu in range(4):
         part = pl.ds(18 * mu, 18)
-        loads.append(pltpu.make_async_copy(u_hbm.at[part], link.at[part], in_sem.at[1 + mu]))
-    loads.append(pltpu.make_async_copy(c_hbm, clov, in_sem.at[5]))
+        groups.append((u_hbm.at[part], link_in.at[part]))
+    groups.append((c_hbm, clov_in))
     for n in (0, 4, 3, 1, 2, 5):
-        loads[n].start()
+        for src, dst in parts_of(*groups[n]):
+            pltpu.make_async_copy(src, dst, in_sem.at[n]).start()
+
+    def arrived(n):
+        held = groups[n][1]
+        pltpu.make_async_copy(held, held, in_sem.at[n]).wait()
+
+    results = [(out_hbm, phi_out)]
+    for mu in range(4):
+        part = pl.ds(18 * mu, 18)
+        results.append((force_hbm.at[part], force_out.at[part]))
+
+    def leave(n):
+        for dst, src in parts_of(*results[n]):
+            pltpu.make_async_copy(src, dst, out_sem.at[n]).start()
+
+    def left(n):
+        held = results[n][1]
+        pltpu.make_async_copy(held, held, out_sem.at[n]).wait()
 
     def window(v):
         return pl.ds(pl.multiple_of(v * TILE, TILE), TILE)
@@ -187,8 +217,8 @@
         store_half(hp, mu, at, ahead)
         store_half(bl, mu, at, mat_vec(load_link(mu, at), ahead, True))
 
-    loads[0].wait()
-    loads[4].wait()
+    arrived(0)
+    arrived(4)
     for_each(chunks, lambda v: project(3, v))
 
     for c in range(12):
@@ -197,7 +227,7 @@
     pl.semaphore_wait(barrier, 4)
     sends[0].start()
     sends[1].start()
-    loads[3].wait()
+    arrived(3)
     for_each(chunks, lambda v: project(2, v))
     for c in range(12):
         face_out[2, c, 0:face_z, :] = hm[2, c, pl.ds(0, face_z, nz), :]
@@ -205,9 +235,9 @@
     sends[2].start()
     sends[3].start()
 
-    loads[1].wait()
+    arrived(1)
     for_each(chunks, lambda v: project(0, v))
-    loads[2].wait()
+    arrived(2)
     for_each(chunks, lambda v: project(1, v))
 
     def shifts(c):
@@ -230,7 +260,7 @@
 
     zero = jnp.zeros((TILE, LANES), jnp.float32)
 
-    loads[5].wait()
+    arrived(5)
 
     def local(v):
         at = window(v)
@@ -288,6 +318,8 @@
     sends[4].start()
     sends[5].start()
 
+    leave(0)
+
     def shifts_phi(c):
         sh_hphi[0, c] = shift_x1(hphi[0, c], 1)
         sh_hphi[1, c] = shift_x2(hphi[1, c], 1)
@@ -324,41 +356,37 @@
                 force_ref[base + 9 + 3 * a + b, at, :] = im
                 force_ref[base + 9 + 3 * b + a, at, :] = im
 
-    for_each(chunks, lambda v: force(0, v))
-    for_each(chunks, lambda v: force(1, v))
+    for mu in (0, 1):
+        for_each(chunks, lambda v: force(mu, v))
+        leave(1 + mu)
 
     for k in (4, 5):
         sends[k].wait_recv()
     for c in range(12):
         sh_hphi[3, c, pl.ds(rows - face_t, face_t), :] = face_in[4, c, 0:face_t, :] * high_sign
         sh_hphi[2, c, pl.ds(nz - 1, face_z, nz), :] = face_in[5, c, 0:face_z, :]
-    for_each(chunks, lambda v: force(2, v))
-    for_each(chunks, lambda v: force(3, v))
+    for mu in (2, 3):
+        for_each(chunks, lambda v: force(mu, v))
+        leave(1 + mu)
     for k in range(6):
         sends[k].wait_send()
-
-
-def to_rows(array):
-    nt, nz, plane = array.shape[-3:]
-    parts = plane // LANES
-    grid = array.reshape((-1, nt, nz, parts, LANES))
-    return jnp.swapaxes(grid, 2, 3).reshape((-1, nt * parts * nz, LANES))
-
-
-def from_rows(rows, shape):
-    nt, nz, plane = shape[-3:]
-    grid = rows.reshape((-1, nt, plane // LANES, nz, LANES))
-    return jnp.swapaxes(grid, 2, 3).reshape(shape)
+    for n in range(5):
+        left(n)
 
 
 def body(spinor, links, clover):
     nt, nz = spinor.shape[3], spinor.shape[4]
-    x, u, c = to_rows(spinor), to_rows(links), to_rows(clover)
-    rows = x.shape[1]
+    sites = spinor.shape[-3:]
+    x, u, c = (a.reshape((-1,) + sites) for a in (spinor, links, clover))
+    parts = nt * (sites[2] // LANES)
+    rows = parts * nz
     face = max(rows // nt, rows // nz)
 
     def halves():
         return pltpu.VMEM((4, 12, rows, LANES), jnp.float32)
+
+    def held(array):
+        return pltpu.VMEM((array.shape[0], parts, nz, LANES), jnp.float32)
 
     applied, force = pl.pallas_call(
         lambda *refs: kernel(nt, nz, *refs),
@@ -368,23 +396,22 @@
             jax.ShapeDtypeStruct(u.shape, jnp.float32),
         ),
         in_specs=[pl.BlockSpec(memory_space=pl.ANY)] * 3,
-        out_specs=(pl.BlockSpec(memory_space=pltpu.VMEM),) * 2,
+        out_specs=(pl.BlockSpec(memory_space=pl.ANY),) * 2,
         scratch_shapes=[
-            pltpu.VMEM(x.shape, jnp.float32),
-            pltpu.VMEM(u.shape, jnp.float32),
-            pltpu.VMEM(c.shape, jnp.float32),
+            held(x), held(u), held(c), held(x), held(u),
             halves(), halves(), halves(), halves(), halves(), halves(),
-            pltpu.VMEM(x.shape, jnp.float32),
+            pltpu.VMEM((24, rows, LANES), jnp.float32),
             halves(), halves(),
             pltpu.VMEM((6, 12, face, LANES), jnp.float32),
             pltpu.VMEM((6, 12, face, LANES), jnp.float32),
             pltpu.SemaphoreType.DMA((6,)),
+            pltpu.SemaphoreType.DMA((5,)),
             pltpu.SemaphoreType.DMA((6,)),
             pltpu.SemaphoreType.DMA((6,)),
         ],
         compiler_params=pltpu.CompilerParams(collective_id=0, has_side_effects=True),
     )(x, u, c)
-    return from_rows(applied, spinor.shape), from_rows(force, links.shape)
+    return applied.reshape(spinor.shape), force.reshape(links.shape)
 
 
 def solution(mesh):

time: 28.3 us -> 20.5 us (0.72)
  local copies, waits for them, and re-layouts: 11.7 us -> 4.09 us
  Pallas kernels: 15.8 us -> 15.5 us
    reshape x7 -> x0, local copies, waits for them, and re-layouts: 7.31 us -> none  [the longest x3 3.59 us: to_rows(): grid = array.reshape((-1, nt, nz, parts, LANES))]
    transpose x3 -> x0, local copies, waits for them, and re-layouts: 4.39 us -> none  [to_rows(): return jnp.swapaxes(grid, 2, 3).reshape((-1, nt * parts * nz, LANES))]
    unnamed x6 -> x2, local copies, waits for them, and re-layouts: 0.01 us -> 4.09 us
where the time goes in v2:
time: 20.5 us; the launch traced here: 20.3 us
  Pallas kernels  15.5 us (76%)
  local copies, waits for them, and re-layouts  4.09 us (20%)
  between operations  0.64 us (3%)
    pallas_call x1, Pallas kernels, body(): pl.pallas_call(lambda *refs: kernel(nt, nz, *refs), name='wilson', out_sh...  15.5 us
    unnamed x2, local copies, waits for them, and re-layouts  4.09 us

profile of v2, /device:TPU:1, one launch (start us, length us, event | category | flops | bytes accessed | tf_op | source)
XLA Modules:
  0.0 20.3 jit_solution(14099582451317171863)
XLA Ops:
  0.6 15.5 %wilson.1 = (f32[24,2,2,768]{3,2,1,0:T(2,128)}, f32[72,2,2,768]{3,2,1,0:T(2,128)}) custom-call(f32[24,2,2,768]{3,2,1,0:T(2,128)} %bitcast.8, f32[72,2,2,768]{3,2,1,0:T(2,128)} %bitcast.6, f32[144,2,2,768]{3,2,1,0:T(2,128)} %bitcast.5), custom_call_target="tpu_custom_call" | custom-call | tf_op jit(solution)/shard_map/wilson/pallas_call | solution.py:391
  16.2 1.7 %copy.7 = f32[2,4,3,2,2,768]{5,4,3,2,1,0:T(2,128)} copy(f32[2,4,3,2,2,768]{5,4,3,2,1,0:T(2,128)} %bitcast.9) | data formatting | bytes 589824
  17.9 2.4 %copy.8 = f32[4,2,3,3,2,2,768]{6,5,4,3,2,1,0:T(2,128)} copy(f32[4,2,3,3,2,2,768]{6,5,4,3,2,1,0:T(2,128)} %bitcast.7) | data formatting | bytes 1769472

commit v3 on v2

--- a/solution.py
+++ b/solution.py
@@ -115,7 +115,7 @@
         part = pl.ds(18 * mu, 18)
         groups.append((u_hbm.at[part], link_in.at[part]))
     groups.append((c_hbm, clov_in))
-    for n in (0, 4, 3, 1, 2, 5):
+    for n in (0, 3, 4, 1, 2, 5):
         for src, dst in parts_of(*groups[n]):
             pltpu.make_async_copy(src, dst, in_sem.at[n]).start()
 
@@ -217,23 +217,30 @@
         store_half(hp, mu, at, ahead)
         store_half(bl, mu, at, mat_vec(load_link(mu, at), ahead, True))
 
+    def face(k, c, size):
+        return k, pl.ds(c * size, size)
+
     arrived(0)
+    arrived(3)
+    for_each(chunks, lambda v: project(2, v))
+    for c in range(12):
+        k, at = face(3, c, face_z)
+        face_out[k, at, :] = bl[2, c, pl.ds(nz - 1, face_z, nz), :]
+    pl.semaphore_wait(barrier, 4)
+    sends[3].start()
+    for c in range(12):
+        k, at = face(2, c, face_z)
+        face_out[k, at, :] = hm[2, c, pl.ds(0, face_z, nz), :]
     arrived(4)
     for_each(chunks, lambda v: project(3, v))
-
-    for c in range(12):
-        face_out[0, c, 0:face_t, :] = hm[3, c, 0:face_t, :]
-        face_out[1, c, 0:face_t, :] = bl[3, c, rows - face_t:rows, :]
-    pl.semaphore_wait(barrier, 4)
+    for c in range(12):
+        k, at = face(0, c, face_t)
+        face_out[k, at, :] = hm[3, c, 0:face_t, :]
+        k, at = face(1, c, face_t)
+        face_out[k, at, :] = bl[3, c, rows - face_t:rows, :]
+    sends[1].start()
     sends[0].start()
-    sends[1].start()
-    arrived(3)
-    for_each(chunks, lambda v: project(2, v))
-    for c in range(12):
-        face_out[2, c, 0:face_z, :] = hm[2, c, pl.ds(0, face_z, nz), :]
-        face_out[3, c, 0:face_z, :] = bl[2, c, pl.ds(nz - 1, face_z, nz), :]
     sends[2].start()
-    sends[3].start()
 
     arrived(1)
     for_each(chunks, lambda v: project(0, v))
@@ -284,16 +291,18 @@
 
     for_each(chunks, local)
 
-    for k in range(4):
+    for k in (0, 1, 3):
         sends[k].wait_recv()
-
-    for c in range(12):
-        sh_hm[3, c, pl.ds(rows - face_t, face_t), :] = face_in[0, c, 0:face_t, :] * high_sign
-        sh_bl[3, c, pl.ds(0, face_t), :] = face_in[1, c, 0:face_t, :] * low_sign
-        sh_hm[2, c, pl.ds(nz - 1, face_z, nz), :] = face_in[2, c, 0:face_z, :]
-        sh_bl[2, c, pl.ds(0, face_z, nz), :] = face_in[3, c, 0:face_z, :]
-
-    def finish(v):
+    for c in range(12):
+        k, at = face(0, c, face_t)
+        sh_hm[3, c, pl.ds(rows - face_t, face_t), :] = face_in[k, at, :] * high_sign
+        k, at = face(1, c, face_t)
+        sh_bl[3, c, pl.ds(0, face_t), :] = face_in[k, at, :] * low_sign
+        k, at = face(3, c, face_z)
+        sh_bl[2, c, pl.ds(0, face_z, nz), :] = face_in[k, at, :]
+        sh_hm[2, c, pl.ds(nz - 1, face_z, nz), :] = jnp.zeros((face_z, LANES), jnp.float32)
+
+    def finish(v, early):
         at = window(v)
         total = [[(zero, zero)] * 3 for _ in range(4)]
         for mu in (2, 3):
@@ -303,6 +312,9 @@
             [(held[s][c][0] - 0.5 * total[s][c][0], held[s][c][1] - 0.5 * total[s][c][1]) for c in range(3)]
             for s in range(4)
         ]
+        if early:
+            store_half(hphi, 2, at, half(2, phi, 1.0))
+            return
         for s in range(4):
             for c in range(3):
                 out_ref[3 * s + c, at, :] = phi[s][c][0]
@@ -310,14 +322,21 @@
         for mu in range(4):
             store_half(hphi, mu, at, half(mu, phi, 1.0))
 
-    for_each(chunks, finish)
-
-    for c in range(12):
-        face_out[4, c, 0:face_t, :] = hphi[3, c, 0:face_t, :]
-        face_out[5, c, 0:face_z, :] = hphi[2, c, pl.ds(0, face_z, nz), :]
+    for_each(chunks, lambda v: finish(v, True))
+    for c in range(12):
+        k, at = face(5, c, face_z)
+        face_out[k, at, :] = hphi[2, c, pl.ds(0, face_z, nz), :]
+    sends[5].start()
+
+    sends[2].wait_recv()
+    for c in range(12):
+        k, at = face(2, c, face_z)
+        sh_hm[2, c, pl.ds(nz - 1, face_z, nz), :] = face_in[k, at, :]
+    for_each(chunks, lambda v: finish(v, False))
+    for c in range(12):
+        k, at = face(4, c, face_t)
+        face_out[k, at, :] = hphi[3, c, 0:face_t, :]
     sends[4].start()
-    sends[5].start()
-
     leave(0)
 
     def shifts_phi(c):
@@ -360,14 +379,18 @@
         for_each(chunks, lambda v: force(mu, v))
         leave(1 + mu)
 
-    for k in (4, 5):
-        sends[k].wait_recv()
-    for c in range(12):
-        sh_hphi[3, c, pl.ds(rows - face_t, face_t), :] = face_in[4, c, 0:face_t, :] * high_sign
-        sh_hphi[2, c, pl.ds(nz - 1, face_z, nz), :] = face_in[5, c, 0:face_z, :]
-    for mu in (2, 3):
-        for_each(chunks, lambda v: force(mu, v))
-        leave(1 + mu)
+    sends[4].wait_recv()
+    for c in range(12):
+        k, at = face(4, c, face_t)
+        sh_hphi[3, c, pl.ds(rows - face_t, face_t), :] = face_in[k, at, :] * high_sign
+    for_each(chunks, lambda v: force(3, v))
+    leave(4)
+    sends[5].wait_recv()
+    for c in range(12):
+        k, at = face(5, c, face_z)
+        sh_hphi[2, c, pl.ds(nz - 1, face_z, nz), :] = face_in[k, at, :]
+    for_each(chunks, lambda v: force(2, v))
+    leave(3)
     for k in range(6):
         sends[k].wait_send()
     for n in range(5):
@@ -402,8 +425,8 @@
             halves(), halves(), halves(), halves(), halves(), halves(),
             pltpu.VMEM((24, rows, LANES), jnp.float32),
             halves(), halves(),
-            pltpu.VMEM((6, 12, face, LANES), jnp.float32),
-            pltpu.VMEM((6, 12, face, LANES), jnp.float32),
+            pltpu.VMEM((6, 12 * face, LANES), jnp.float32),
+            pltpu.VMEM((6, 12 * face, LANES), jnp.float32),
             pltpu.SemaphoreType.DMA((6,)),
             pltpu.SemaphoreType.DMA((5,)),
             pltpu.SemaphoreType.DMA((6,)),

time: 20.5 us -> 19.2 us (0.937)
  Pallas kernels: 15.5 us -> 14.3 us
    pallas_call x1, Pallas kernels: 15.5 us -> 14.3 us  [body(): pl.pallas_call(lambda *refs: kernel(nt, nz, *refs), name='wilson', out_sh...]
where the time goes in v3:
time: 19.2 us; the launch traced here: 19 us
  Pallas kernels  14.3 us (74%)
  local copies, waits for them, and re-layouts  4.09 us (21%)
  between operations  0.64 us (3%)
    pallas_call x1, Pallas kernels, body(): pl.pallas_call(lambda *refs: kernel(nt, nz, *refs), name='wilson', out_sh...  14.3 us
    unnamed x2, local copies, waits for them, and re-layouts  4.09 us

profile of v3, /device:TPU:1, one launch (start us, length us, event | category | flops | bytes accessed | tf_op | source)
XLA Modules:
  0.0 19.0 jit_solution(10658457906040395058)
XLA Ops:
  0.6 14.3 %wilson.1 = (f32[24,2,2,768]{3,2,1,0:T(2,128)}, f32[72,2,2,768]{3,2,1,0:T(2,128)}) custom-call(f32[24,2,2,768]{3,2,1,0:T(2,128)} %bitcast.8, f32[72,2,2,768]{3,2,1,0:T(2,128)} %bitcast.6, f32[144,2,2,768]{3,2,1,0:T(2,128)} %bitcast.5), custom_call_target="tpu_custom_call" | custom-call | tf_op jit(solution)/shard_map/wilson/pallas_call | solution.py:414
  14.9 1.7 %copy.7 = f32[2,4,3,2,2,768]{5,4,3,2,1,0:T(2,128)} copy(f32[2,4,3,2,2,768]{5,4,3,2,1,0:T(2,128)} %bitcast.9) | data formatting | bytes 589824
  16.6 2.4 %copy.8 = f32[4,2,3,3,2,2,768]{6,5,4,3,2,1,0:T(2,128)} copy(f32[4,2,3,3,2,2,768]{6,5,4,3,2,1,0:T(2,128)} %bitcast.7) | data formatting | bytes 1769472
